TPU v7x, 128 devices: a whole 4x4x4 slice. The times are simulated.
128 devices in a mesh: ctx: 8 (over y, core), fsdp: 16 (over x, z).
Axes of the slice: x: 4, y: 4, z: 4, core: 2. Of those that a mesh axis runs over, the one named last changes fastest.
Arguments:
- hidden: bfloat16 [8, 16, 256, 2048], P('ctx', 'fsdp'), may hold values from -4.5 to 4.5
- norm_gain: float32 [2048], replicated, may hold values from 0.1 to 1.9
- w_query: bfloat16 [2048, 2048], P('fsdp', 'ctx'), may hold values from -1 to 1
- w_key: bfloat16 [2048, 1024], P('fsdp', 'ctx'), may hold values from -1 to 1
- w_value: bfloat16 [2048, 1024], P('fsdp', 'ctx'), may hold values from -0.125 to 0.125
- q_gain: float32 [128], replicated, may hold values from 0.5 to 5
- k_gain: float32 [128], replicated, may hold values from 0.5 to 5
- lengths: int32 [16, 4], replicated, may hold values from 1 to 1024, 2048 in all within a row
- piece_map: int32 [16, 8], replicated, may hold values from 0 to 7, each once within a row
- owner: int32 [8, 16, 256], P('ctx', 'fsdp'), may hold values from 0 to 127, as said below
- slot: int32 [8, 16, 256], P('ctx', 'fsdp'), may hold values from 0 to 511, as said below
Outputs:
- attended: bfloat16 [8, 16, 256, 2048], P('ctx', 'fsdp')
- cache: bfloat16 [65536, 2048], P(('ctx', 'fsdp'))
Inputs may be any that keep to these rules, and one draw needn't show every extreme that they name: `lengths`: each row sums to 2048; its largest entry is 1024. `piece_map`: each row holds every piece once. At most 4 tokens of one device go to one owner; in every draw one owner receives exactly 4 from every device. `slot`: tokens with the same owner have distinct slots.
All inputs are finite; a program needn't handle non-finite values.
Results may differ from a plain program's by a relative error of at most 0.0035.
The roundings to bfloat16 on the way count: a program that leaves them out, or rounds other values in their place, can miss the bound.
Values may be sent and summed in bfloat16 or wider, within the bound.
No kernel may reach another device: no remote copies, remote signals or barrier semaphores. Data moves between devices by JAX's collectives and lax.ppermute only.
A program may use at most 128 MiB of HBM per device.

v0:
```python
import math
import jax
import jax.numpy as jnp
from jax import lax
from jax.sharding import PartitionSpec as P

HEAD_WIDTH = 128
EPSILON = 1e-06
THETA = 1000000.0
NEG_BIG = -1e30


def norm_rope(projected, gain_vec, relative, head_size):
    row_count = projected.shape[0]
    head_count = projected.shape[1] // head_size
    shaped = projected.reshape(row_count, head_count, head_size)
    factor = lax.rsqrt(jnp.mean(shaped * shaped, axis=-1, keepdims=True) + EPSILON)
    normal = shaped * factor * gain_vec
    half_size = head_size // 2
    frequency = jnp.exp(
        jnp.arange(half_size, dtype=jnp.float32) * (-2.0 * math.log(THETA) / head_size)
    )
    angles = relative.astype(jnp.float32)[:, None] * frequency[None, :]
    cosine = jnp.cos(angles)[:, None, :]
    sine_part = jnp.sin(angles)[:, None, :]
    first_half = normal[..., :half_size]
    second = normal[..., half_size:]
    turned = jnp.concatenate(
        [first_half * cosine - second * sine_part, second * cosine + first_half * sine_part],
        axis=-1,
    )
    return turned.reshape(row_count, head_count * head_size).astype(jnp.bfloat16)


def attend_keys(
    state_tuple, heads_of_query, query_pos, query_seg, key_rows, value_rows, key_pos, key_seg
):
    row_max, row_sum, weighted = state_tuple
    heads_of_key = key_rows.reshape(key_rows.shape[0], -1, HEAD_WIDTH)
    heads_of_value = value_rows.reshape(value_rows.shape[0], -1, HEAD_WIDTH)
    scores = jnp.einsum(
        "tkgd,skd->tkgs", heads_of_query, heads_of_key, preferred_element_type=jnp.float32
    ) * (1.0 / math.sqrt(HEAD_WIDTH))
    visible = ((query_seg[:, None] == key_seg[None, :]) & (key_pos[None, :] <= query_pos[:, None]))[
        :, None, None, :
    ]
    masked = jnp.where(visible, scores, NEG_BIG)
    new_max = jnp.maximum(row_max, jnp.max(masked, axis=-1))
    weights = jnp.where(visible, jnp.exp(masked - new_max[..., None]), 0.0)
    shrink = jnp.exp(row_max - new_max)
    row_sum = row_sum * shrink + jnp.sum(weights, axis=-1)
    weighted = weighted * shrink[..., None] + jnp.einsum(
        "tkgs,skd->tkgd",
        weights.astype(jnp.bfloat16),
        heads_of_value,
        preferred_element_type=jnp.float32,
    )
    return (new_max, row_sum, weighted)


def sweep_keys(
    state_tuple, heads_of_query, query_pos, query_seg, key_rows, value_rows, key_pos, key_seg
):
    row_span = key_rows.shape[0]
    key_block = 512
    steps_count = row_span // key_block

    def step_keys(carried, key_items):
        return (
            attend_keys(
                carried,
                heads_of_query,
                query_pos,
                query_seg,
                key_items[0],
                key_items[1],
                key_items[2],
                key_items[3],
            ),
            None,
        )

    result_carry, unused = lax.scan(
        step_keys,
        state_tuple,
        (
            key_rows.reshape(steps_count, key_block, -1),
            value_rows.reshape(steps_count, key_block, -1),
            key_pos.reshape(steps_count, key_block),
            key_seg.reshape(steps_count, key_block),
        ),
    )
    return result_carry


def empty_state(row_count, kv_heads, group_width):
    return (
        jnp.full((row_count, kv_heads, group_width), NEG_BIG, jnp.float32),
        jnp.zeros((row_count, kv_heads, group_width), jnp.float32),
        jnp.zeros((row_count, kv_heads, group_width, HEAD_WIDTH), jnp.float32),
    )


def project_rows(source, pieces):
    return tuple(
        (jnp.dot(source, shard_rows, preferred_element_type=jnp.float32) for shard_rows in pieces)
    )


def shards(
    hidden, norm_gain, w_query, w_key, w_value, q_gain, k_gain, lengths, piece_map, owner, slot
):
    tok_rows = hidden.shape[2]
    ctx_count = lax.axis_size("ctx")
    fsdp_count = lax.axis_size("fsdp")
    owner_count = ctx_count * fsdp_count
    group_index = lax.axis_index("fsdp")
    ctx_index = lax.axis_index("ctx")
    inputs = hidden[0, 0].astype(jnp.float32)
    factor = lax.rsqrt(jnp.mean(inputs * inputs, axis=-1, keepdims=True) + EPSILON)
    normed = (inputs * factor * norm_gain).astype(jnp.bfloat16)
    my_lengths = lax.dynamic_index_in_dim(lengths, group_index, 0, keepdims=False)
    my_pieces = lax.dynamic_index_in_dim(piece_map, group_index, 0, keepdims=False)
    seg_ends = jnp.cumsum(my_lengths, dtype=jnp.int32)
    starts = seg_ends - my_lengths
    seg_count = lengths.shape[1]

    def stream_info(row_ids):
        holder = row_ids // tok_rows
        piece_ids = jnp.sum(
            jnp.where(
                holder[:, None] == jnp.arange(ctx_count, dtype=jnp.int32)[None, :],
                my_pieces[None, :],
                0,
            ),
            axis=1,
            dtype=jnp.int32,
        )
        positions = piece_ids * tok_rows + row_ids % tok_rows
        segment = jnp.sum(
            (positions[:, None] >= seg_ends[None, :]).astype(jnp.int32), axis=1, dtype=jnp.int32
        )
        relative = positions - jnp.sum(
            jnp.where(
                segment[:, None] == jnp.arange(seg_count, dtype=jnp.int32)[None, :],
                starts[None, :],
                0,
            ),
            axis=1,
            dtype=jnp.int32,
        )
        return (positions, segment, relative)

    query_cols, key_cols, value_cols = (
        lax.all_gather(w_query, "ctx", axis=1, tiled=True),
        lax.all_gather(w_key, "ctx", axis=1, tiled=True),
        lax.all_gather(w_value, "ctx", axis=1, tiled=True),
    )
    query_raw, key_raw, value_raw = project_rows(
        normed,
        (
            lax.all_gather(query_cols, "fsdp", axis=0, tiled=True),
            lax.all_gather(key_cols, "fsdp", axis=0, tiled=True),
            lax.all_gather(value_cols, "fsdp", axis=0, tiled=True),
        ),
    )
    own_ids = ctx_index * tok_rows + jnp.arange(tok_rows, dtype=jnp.int32)
    own_pos, own_seg, own_rel = stream_info(own_ids)
    query_rows = norm_rope(query_raw, q_gain, own_rel, HEAD_WIDTH)
    key_new = norm_rope(key_raw, k_gain, own_rel, HEAD_WIDTH)
    value_new = value_raw.astype(jnp.bfloat16)
    kv_heads = key_new.shape[1] // HEAD_WIDTH
    group_width = query_rows.shape[1] // key_new.shape[1]
    heads_of_query = query_rows.reshape(tok_rows, kv_heads, group_width, HEAD_WIDTH)
    pieces = (
        lax.all_gather(key_new, "ctx", axis=0, tiled=True),
        lax.all_gather(value_new, "ctx", axis=0, tiled=True),
    )
    row_ids = jnp.arange(pieces[0].shape[0], dtype=jnp.int32)
    key_pos, key_seg, unused = stream_info(row_ids)
    row_max, row_sum, weighted = sweep_keys(
        empty_state(tok_rows, kv_heads, group_width),
        heads_of_query,
        own_pos,
        own_seg,
        pieces[0],
        pieces[1],
        key_pos,
        key_seg,
    )
    attended = (weighted / row_sum[..., None]).reshape(tok_rows, -1).astype(jnp.bfloat16)
    kv_new = jnp.concatenate([key_new, value_new], axis=1)
    kv_width = kv_new.shape[1]
    per_owner = 2 * tok_rows // owner_count
    capacity = owner_count * per_owner
    own_owner = owner[0, 0]
    own_slot = slot[0, 0]
    onehot = (own_owner[:, None] == jnp.arange(owner_count, dtype=jnp.int32)[None, :]).astype(
        jnp.int32
    )
    rank_in_owner = jnp.sum(
        onehot * (jnp.cumsum(onehot, axis=0, dtype=jnp.int32) - 1), axis=1, dtype=jnp.int32
    )
    bucket_pos = own_owner * per_owner + rank_in_owner
    bucket = jnp.zeros((capacity, kv_width), jnp.bfloat16).at[bucket_pos].set(kv_new)
    bucket_slots = jnp.full((capacity,), capacity, jnp.int32).at[bucket_pos].set(own_slot)
    got_rows, got_slots = (
        lax.all_to_all(
            bucket.reshape(owner_count, per_owner, kv_width),
            ("ctx", "fsdp"),
            split_axis=0,
            concat_axis=0,
            tiled=True,
        ),
        lax.all_to_all(
            bucket_slots.reshape(owner_count, per_owner),
            ("ctx", "fsdp"),
            split_axis=0,
            concat_axis=0,
            tiled=True,
        ),
    )
    new_cache = (
        jnp.zeros((capacity, kv_width), jnp.bfloat16)
        .at[got_slots.reshape(-1)]
        .set(got_rows.reshape(-1, kv_width), mode="drop")
    )
    return (attended[None, None], new_cache)


def solution(mesh):
    placed = (
        P("ctx", "fsdp", None, None),
        P(),
        P("fsdp", "ctx"),
        P("fsdp", "ctx"),
        P("fsdp", "ctx"),
        P(),
        P(),
        P(),
        P(),
        P("ctx", "fsdp", None),
        P("ctx", "fsdp", None),
    )
    return jax.shard_map(
        shards,
        mesh=mesh,
        in_specs=placed,
        out_specs=(P("ctx", "fsdp", None, None), P(("ctx", "fsdp"), None)),
        check_vma=False,
    )
```

profile of v0, /device:TPU:1, one launch (start us, length us, event | category | flops | bytes accessed | tf_op | source)
XLA Modules:
  0.0 381.6 jit_solution(15677622843119619807)
XLA Ops:
  7.2 15.2 %all_gather.24 = bf16[128,1024]{1,0:T(8,128)(2,1)} all-gather(bf16[128,128]{1,0:T(8,128)(2,1)} %param.16), channel_id=1, replica_groups=mesh['ctx'=8,'fsdp'=16] {'ctx'}, dimensions={1}, use_global_device_ids=true | all-gather | bytes 294912 | tf_op jit(solution)/shard_map/all_gather | solution.py:156
  22.5 12.6 %all_gather.29 = bf16[128,1024]{1,0:T(8,128)(2,1)} all-gather(bf16[128,128]{1,0:T(8,128)(2,1)} %param.17), channel_id=1, replica_groups=mesh['ctx'=8,'fsdp'=16] {'ctx'}, dimensions={1}, use_global_device_ids=true | all-gather | bytes 294912 | tf_op jit(solution)/shard_map/all_gather | solution.py:157
  35.2 14.4 %all_gather.27 = bf16[128,2048]{1,0:T(8,128)(2,1)} all-gather(bf16[128,256]{1,0:T(8,128)(2,1)} %param.15), channel_id=1, replica_groups=mesh['ctx'=8,'fsdp'=16] {'ctx'}, dimensions={1}, use_global_device_ids=true | all-gather | bytes 589824 | tf_op jit(solution)/shard_map/all_gather | solution.py:155
  51.1 23.9 %all-gather.6.cloned.1.call-done = bf16[2048,1024]{1,0:T(8,128)(2,1)} async-done(((bf16[128,1024]{1,0:T(8,128)(2,1)}), bf16[2048,1024]{1,0:T(8,128)(2,1)}) %all-gather.6.cloned.1.call-update) | async-done | bytes 4194320 | tf_op jit(solution)/shard_map/all_gather | solution.py:163
  75.0 6.5 %copy.64 = bf16[1024,2048]{1,0:T(8,128)(2,1)} copy(bf16[1024,2048]{0,1:T(8,128)(2,1)} %bitcast.121) | data formatting | bytes 8388608 | tf_op jit(solution)/shard_map/dot_general | solution.py:106
  81.5 3.6 multiply_reduce_fusion.1
  86.7 41.8 %all-gather.12.cloned.1.call-done = bf16[2048,1024]{1,0:T(8,128)(2,1)} async-done(((bf16[128,1024]{1,0:T(8,128)(2,1)}), bf16[2048,1024]{1,0:T(8,128)(2,1)}) %all-gather.12.cloned.1.call-update) | async-done | bytes 4194320 | tf_op jit(solution)/shard_map/all_gather | solution.py:164
  128.4 4.3 %convolution_convert_fusion = bf16[256,1024]{1,0:T(8,128)(2,1)} fusion(bf16[2048,1024]{1,0:T(8,128)(2,1)} %all-gather.12.cloned.1.call-done, bf16[1,1,256,2048]{3,2,1,0:T(8,128)(2,1)S(1)} %copy-done.3, f32[2048]{0:T(1024)S(1)} %copy-done.9, f32[256]{0:T(256)S(1)} %add_rsqrt_fusion.2), kind=kOutput, calls=%fused_computation.37 | convolution fusion | flops 1076101120 | bytes 5776384 | tf_op jit(solution)/shard_map/dot_general | solution.py:106
  135.7 7.9 %all-to-all-start = ((s32[128,1,4]{2,1,0:T(1,128)}), s32[128,1,4]{2,1,0:T(1,128)S(1)}, u32[]{:S(2)}, u32[]{:S(2)}) async-start(s32[128,1,4]{2,1,0:T(1,128)} %bitcast.26), calls=%async_computation | async-start | bytes 131072 | tf_op jit(solution)/shard_map/all_to_all | solution.py:215
  143.6 3.3 scatter_custom_fusion.1
  149.1 4.1 %all-to-all-done = s32[128,1,4]{2,1,0:T(1,128)S(1)} async-done(((s32[128,1,4]{2,1,0:T(1,128)}), s32[128,1,4]{2,1,0:T(1,128)S(1)}, u32[]{:S(2)}, u32[]{:S(2)}) %all-to-all-start) | async-done | bytes 2080 | tf_op jit(solution)/shard_map/all_to_all | solution.py:215
  153.2 5.7 %all-to-all-start.1 = ((bf16[128,4,2048]{2,1,0:T(4,128)(2,1)}), bf16[128,4,2048]{2,1,0:T(4,128)(2,1)S(1)}, u32[]{:S(2)}, u32[]{:S(2)}) async-start(bf16[128,4,2048]{2,1,0:T(4,128)(2,1)} %reshape.385), calls=%async_computation.1 | async-start | bytes 4194304 | tf_op jit(solution)/shard_map/all_to_all | solution.py:208
  160.7 45.7 %all-to-all-done.1 = bf16[128,4,2048]{2,1,0:T(4,128)(2,1)S(1)} async-done(((bf16[128,4,2048]{2,1,0:T(4,128)(2,1)}), bf16[128,4,2048]{2,1,0:T(4,128)(2,1)S(1)}, u32[]{:S(2)}, u32[]{:S(2)}) %all-to-all-start.1) | async-done | bytes 2097184 | tf_op jit(solution)/shard_map/all_to_all | solution.py:208
  208.4 6.2 %scatter_custom_fusion.2 = bf16[512,2048]{1,0:T(8,128)(2,1)} fusion(s32[512]{0:T(512)S(1)} %bitcast.132, bf16[512,2048]{1,0:T(8,128)(2,1)} %reshape.408, bf16[]{:T(256)} %constant.129.clone.1), kind=kCustom, calls=%fused_computation.44 | custom fusion | bytes 2097664 | tf_op jit(solution)/shard_map/scatter | solution.py:226
  214.7 5.5 %all-gather.10.cloned.1.call-done = bf16[2048,2048]{1,0:T(8,128)(2,1)} async-done(((bf16[128,2048]{1,0:T(8,128)(2,1)}), bf16[2048,2048]{1,0:T(8,128)(2,1)}) %all-gather.10.cloned.1.call-update) | async-done | bytes 8388624 | tf_op jit(solution)/shard_map/all_gather | solution.py:162
  220.1 12.5 %copy.66 = bf16[2048,2048]{1,0:T(8,128)(2,1)} copy(bf16[2048,2048]{0,1:T(8,128)(2,1)} %bitcast.116) | data formatting | bytes 16777216 | tf_op jit(solution)/shard_map/dot_general | solution.py:106
  232.6 6.0 %multiply_reduce_fusion = (f32[256,16]{0,1:T(8,128)S(1)}, f32[256,16,128]{0,2,1:T(8,128)S(1)}) fusion(bf16[16,128,2048]{2,1,0:T(8,128)(2,1)} %bitcast.117, bf16[1,1,256,2048]{3,2,1,0:T(8,128)(2,1)S(1)} %copy-done.4, f32[2048]{0:T(1024)S(1)} %copy-done.9, f32[256]{0:T(256)S(1)} %add_rsqrt_fusion.2), kind=kOutput, calls=%fused_computation.36 | convolution fusion | flops 2150625280 | bytes 11559936 | tf_op jit(solution)/shard_map/dot_general | solution.py:106
  240.7 12.2 %all-gather.8.cloned.1.call-done = bf16[2048,1024]{1,0:T(8,128)(2,1)} async-done(((bf16[256,1024]{1,0:T(8,128)(2,1)}), bf16[2048,1024]{1,0:T(8,128)(2,1)}) %all-gather.8.cloned.1.call-update) | async-done | bytes 4194320 | tf_op jit(solution)/shard_map/all_gather | solution.py:176
  253.0 33.7 %all-gather.14.cloned.1.call-done = bf16[2048,1024]{1,0:T(8,128)(2,1)} async-done(((bf16[256,1024]{1,0:T(8,128)(2,1)}), bf16[2048,1024]{1,0:T(8,128)(2,1)}) %all-gather.14.cloned.1.call-update) | async-done | bytes 4194320 | tf_op jit(solution)/shard_map/all_gather | solution.py:177
  286.6 85.2 %while.15 = (s32[]{:T(128)}, f32[256,8,2]{0,2,1:T(2,128)S(1)}, f32[256,8,2]{0,2,1:T(2,128)S(1)}, f32[256,8,2,128]{0,3,2,1:T(8,128)}, s32[256]{0:T(256)S(1)}, /*i...) while((s32[]{:T(128)}, f32[256,8,2]{0,2,1:T(2,128)S(1)}, ...), condition=%wide.region_12.13_spmd.clone, body=%wide.region_9.12_spmd.clone.sunk | while | flops 1102991360 | bytes 41695372 | solution.py:83
  289.1 6.0 %fusion.72 = (f32[256,8,2]{0,2,1:T(2,128)S(1)}, f32[8,512,256,2]{2,1,3,0:T(8,128)}) fusion(pred[256,512]{0,1:T(8,128)(4,1)S(1)} %compare_and_fusion.2, bf16[512,8,128,1]{0,2,3,1:T(8,128)(2,1)S(1)} %bitcast.114, bf16[256,8,2,128]{3,0,2,1:T(8,128)(2,1)} %get-tuple-element.313), kind=kOutput, calls=%fused_computation.5.clone.1 | convolution fusion | flops 543158272 | bytes 10633216 | tf_op jit(solution)/shard_map/while/body/eval_jaxpr/tkgd,skd->tkgs/dot_general | solution.py:41
  295.2 4.5 %fusion.74 = f32[256,8,2]{0,2,1:T(2,128)S(1)} fusion(f32[8,512,256,2]{2,1,3,0:T(8,128)} %get-tuple-element.274, f32[256,8,2]{0,2,1:T(2,128)S(1)} %fusion.73, pred[256,512]{0,1:T(8,128)(4,1)S(1)} %compare_and_fusion.2), kind=kLoop, calls=%fused_computation.7.clone.1 | loop fusion | flops 10481664 | bytes 8552448 | tf_op jit(solution)/shard_map/while/body/eval_jaxpr/reduce_sum | solution.py:51
  300.2 7.2 %bitcast_add_fusion.3 = f32[256,8,2,128]{0,3,2,1:T(8,128)} fusion(f32[256,8,2,128]{0,3,2,1:T(8,128)} %get-tuple-element.294, bf16[512,8,128,1]{0,2,3,1:T(8,128)(2,1)S(1)} %bitcast.115, f32[8,512,256,2]{2,1,3,0:T(8,128)} %get-tuple-element.274, f32[256,8,2]{0,2,1:T(2,128)S(1)} %fusion.73, pred[256,512]{0,1:T(8,128)(4,1)S(1)} %compare_and_fusion.2, ...), kind=kOutput, calls=%fused_computation.10.clone.1 | convolution fusion | flops 548929536 | bytes 13795329 | tf_op jit(solution)/shard_map/while/body/eval_jaxpr/tkgs,skd->tkgd/dot_general | solution.py:52
  310.0 6.0 %fusion.72 = (f32[256,8,2]{0,2,1:T(2,128)S(1)}, f32[8,512,256,2]{2,1,3,0:T(8,128)}) fusion(pred[256,512]{0,1:T(8,128)(4,1)S(1)} %compare_and_fusion.2, bf16[512,8,128,1]{0,2,3,1:T(8,128)(2,1)S(1)} %bitcast.114, bf16[256,8,2,128]{3,0,2,1:T(8,128)(2,1)} %get-tuple-element.313), kind=kOutput, calls=%fused_computation.5.clone.1 | convolution fusion | flops 543158272 | bytes 10633216 | tf_op jit(solution)/shard_map/while/body/eval_jaxpr/tkgd,skd->tkgs/dot_general | solution.py:41
  316.0 4.5 %fusion.74 = f32[256,8,2]{0,2,1:T(2,128)S(1)} fusion(f32[8,512,256,2]{2,1,3,0:T(8,128)} %get-tuple-element.274, f32[256,8,2]{0,2,1:T(2,128)S(1)} %fusion.73, pred[256,512]{0,1:T(8,128)(4,1)S(1)} %compare_and_fusion.2), kind=kLoop, calls=%fused_computation.7.clone.1 | loop fusion | flops 10481664 | bytes 8552448 | tf_op jit(solution)/shard_map/while/body/eval_jaxpr/reduce_sum | solution.py:51
  321.1 7.8 %bitcast_add_fusion.3 = f32[256,8,2,128]{0,3,2,1:T(8,128)} fusion(f32[256,8,2,128]{0,3,2,1:T(8,128)} %get-tuple-element.294, bf16[512,8,128,1]{0,2,3,1:T(8,128)(2,1)S(1)} %bitcast.115, f32[8,512,256,2]{2,1,3,0:T(8,128)} %get-tuple-element.274, f32[256,8,2]{0,2,1:T(2,128)S(1)} %fusion.73, pred[256,512]{0,1:T(8,128)(4,1)S(1)} %compare_and_fusion.2, ...), kind=kOutput, calls=%fused_computation.10.clone.1 | convolution fusion | flops 548929536 | bytes 13795329 | tf_op jit(solution)/shard_map/while/body/eval_jaxpr/tkgs,skd->tkgd/dot_general | solution.py:52
  331.4 6.0 %fusion.72 = (f32[256,8,2]{0,2,1:T(2,128)S(1)}, f32[8,512,256,2]{2,1,3,0:T(8,128)}) fusion(pred[256,512]{0,1:T(8,128)(4,1)S(1)} %compare_and_fusion.2, bf16[512,8,128,1]{0,2,3,1:T(8,128)(2,1)S(1)} %bitcast.114, bf16[256,8,2,128]{3,0,2,1:T(8,128)(2,1)} %get-tuple-element.313), kind=kOutput, calls=%fused_computation.5.clone.1 | convolution fusion | flops 543158272 | bytes 10633216 | tf_op jit(solution)/shard_map/while/body/eval_jaxpr/tkgd,skd->tkgs/dot_general | solution.py:41
  337.5 4.5 %fusion.74 = f32[256,8,2]{0,2,1:T(2,128)S(1)} fusion(f32[8,512,256,2]{2,1,3,0:T(8,128)} %get-tuple-element.274, f32[256,8,2]{0,2,1:T(2,128)S(1)} %fusion.73, pred[256,512]{0,1:T(8,128)(4,1)S(1)} %compare_and_fusion.2), kind=kLoop, calls=%fused_computation.7.clone.1 | loop fusion | flops 10481664 | bytes 8552448 | tf_op jit(solution)/shard_map/while/body/eval_jaxpr/reduce_sum | solution.py:51
  342.5 7.8 %bitcast_add_fusion.3 = f32[256,8,2,128]{0,3,2,1:T(8,128)} fusion(f32[256,8,2,128]{0,3,2,1:T(8,128)} %get-tuple-element.294, bf16[512,8,128,1]{0,2,3,1:T(8,128)(2,1)S(1)} %bitcast.115, f32[8,512,256,2]{2,1,3,0:T(8,128)} %get-tuple-element.274, f32[256,8,2]{0,2,1:T(2,128)S(1)} %fusion.73, pred[256,512]{0,1:T(8,128)(4,1)S(1)} %compare_and_fusion.2, ...), kind=kOutput, calls=%fused_computation.10.clone.1 | convolution fusion | flops 548929536 | bytes 13795329 | tf_op jit(solution)/shard_map/while/body/eval_jaxpr/tkgs,skd->tkgd/dot_general | solution.py:52
  352.9 6.0 %fusion.72 = (f32[256,8,2]{0,2,1:T(2,128)S(1)}, f32[8,512,256,2]{2,1,3,0:T(8,128)}) fusion(pred[256,512]{0,1:T(8,128)(4,1)S(1)} %compare_and_fusion.2, bf16[512,8,128,1]{0,2,3,1:T(8,128)(2,1)S(1)} %bitcast.114, bf16[256,8,2,128]{3,0,2,1:T(8,128)(2,1)} %get-tuple-element.313), kind=kOutput, calls=%fused_computation.5.clone.1 | convolution fusion | flops 543158272 | bytes 10633216 | tf_op jit(solution)/shard_map/while/body/eval_jaxpr/tkgd,skd->tkgs/dot_general | solution.py:41
  358.9 4.5 %fusion.74 = f32[256,8,2]{0,2,1:T(2,128)S(1)} fusion(f32[8,512,256,2]{2,1,3,0:T(8,128)} %get-tuple-element.274, f32[256,8,2]{0,2,1:T(2,128)S(1)} %fusion.73, pred[256,512]{0,1:T(8,128)(4,1)S(1)} %compare_and_fusion.2), kind=kLoop, calls=%fused_computation.7.clone.1 | loop fusion | flops 10481664 | bytes 8552448 | tf_op jit(solution)/shard_map/while/body/eval_jaxpr/reduce_sum | solution.py:51
  364.0 7.8 %bitcast_add_fusion.3 = f32[256,8,2,128]{0,3,2,1:T(8,128)} fusion(f32[256,8,2,128]{0,3,2,1:T(8,128)} %get-tuple-element.294, bf16[512,8,128,1]{0,2,3,1:T(8,128)(2,1)S(1)} %bitcast.115, f32[8,512,256,2]{2,1,3,0:T(8,128)} %get-tuple-element.274, f32[256,8,2]{0,2,1:T(2,128)S(1)} %fusion.73, pred[256,512]{0,1:T(8,128)(4,1)S(1)} %compare_and_fusion.2, ...), kind=kOutput, calls=%fused_computation.10.clone.1 | convolution fusion | flops 548929536 | bytes 13795329 | tf_op jit(solution)/shard_map/while/body/eval_jaxpr/tkgs,skd->tkgd/dot_general | solution.py:52
  (116 shorter events, 29.7 us)
Async XLA Ops:
  7.2 42.5 %copy-start = (s32[16,8]{0,1:T(8,128)S(1)}, s32[16,8]{0,1:T(8,128)}, u32[]{:S(2)}) copy-start(s32[16,8]{0,1:T(8,128)} %param.21) | copy-start | bytes 1540
  7.2 42.7 %copy-start.6 = (s32[16,4]{0,1:T(4,128)S(1)}, s32[16,4]{0,1:T(4,128)}, u32[]{:S(2)}) copy-start(s32[16,4]{0,1:T(4,128)} %param.20) | copy-start | bytes 772
  7.2 43.3 %copy-start.3 = (bf16[1,1,256,2048]{3,2,1,0:T(8,128)(2,1)S(1)}, bf16[1,1,256,2048]{3,2,1,0:T(8,128)(2,1)}, u32[]{:S(2)}) copy-start(bf16[1,1,256,2048]{3,2,1,0:T(8,128)(2,1)} %param.13) | copy-start | bytes 3145732
  7.2 67.8 %all-gather.6.cloned.1.call-start = ((), (), s32[]{:S(2)}) async-start(), calls=%async_computation.2 | async-start | bytes 4456448 | tf_op jit(solution)/shard_map/all_gather | solution.py:163
  22.5 106.0 %all-gather.12.cloned.1.call-start = ((), (), s32[]{:S(2)}) async-start(), calls=%async_computation.5 | async-start | bytes 4456448 | tf_op jit(solution)/shard_map/all_gather | solution.py:164
  35.1 185.0 %all-gather.10.cloned.1.call-start = ((), (), s32[]{:S(2)}) async-start(), calls=%async_computation.4 | async-start | bytes 8912896 | tf_op jit(solution)/shard_map/all_gather | solution.py:162
  49.6 203.4 %all-gather.8.cloned.1.call-start = ((), (), s32[]{:S(2)}) async-start(), calls=%async_computation.3 | async-start | bytes 4718592 | tf_op jit(solution)/shard_map/all_gather | solution.py:176
  75.0 6.5 %copy-start.9 = (f32[2048]{0:T(1024)S(1)}, f32[2048]{0:T(1024)}, u32[]{:S(2)}) copy-start(f32[2048]{0:T(1024)} %param.14) | copy-start | bytes 24580
  81.5 3.6 copy-start.7
  86.6 46.1 %copy-start.5 = (s32[1,1,256]{2,1,0:T(1,128)S(1)}, s32[1,1,256]{2,1,0:T(1,128)}, u32[]{:S(2)}) copy-start(s32[1,1,256]{2,1,0:T(1,128)} %param.22) | copy-start | bytes 3076
  86.6 57.0 %copy-start.2 = (bf16[256,1024]{1,0:T(8,128)(2,1)S(1)}, bf16[256,1024]{1,0:T(8,128)(2,1)}, u32[]{:S(2)}) copy-start(bf16[256,1024]{1,0:T(8,128)(2,1)} %copy.65) | copy-start | bytes 1572868
  86.6 200.0 %all-gather.14.cloned.1.call-start = ((), (), s32[]{:S(2)}) async-start(), calls=%async_computation.6 | async-start | bytes 4718592 | tf_op jit(solution)/shard_map/all_gather | solution.py:177
  135.7 17.5 %all-to-all-start = ((s32[128,1,4]{2,1,0:T(1,128)}), s32[128,1,4]{2,1,0:T(1,128)S(1)}, u32[]{:S(2)}, u32[]{:S(2)}) async-start(s32[128,1,4]{2,1,0:T(1,128)} %bitcast.26), calls=%async_computation | async-start | bytes 131072 | tf_op jit(solution)/shard_map/all_to_all | solution.py:215
  153.2 53.2 %all-to-all-start.1 = ((bf16[128,4,2048]{2,1,0:T(4,128)(2,1)}), bf16[128,4,2048]{2,1,0:T(4,128)(2,1)S(1)}, u32[]{:S(2)}, u32[]{:S(2)}) async-start(bf16[128,4,2048]{2,1,0:T(4,128)(2,1)} %reshape.385), calls=%async_computation.1 | async-start | bytes 4194304 | tf_op jit(solution)/shard_map/all_to_all | solution.py:208
  220.1 12.5 %copy-start.4 = (bf16[1,1,256,2048]{3,2,1,0:T(8,128)(2,1)S(1)}, bf16[1,1,256,2048]{3,2,1,0:T(8,128)(2,1)}, u32[]{:S(2)}) copy-start(bf16[1,1,256,2048]{3,2,1,0:T(8,128)(2,1)} %param.13) | copy-start | bytes 3145732
  232.6 6.0 %copy-start.8 = (f32[128]{0:T(128)S(1)}, f32[128]{0:T(128)}, u32[]{:S(2)}) copy-start(f32[128]{0:T(128)} %param.18) | copy-start | bytes 1540
  371.8 3.2 copy-start.1
Sparse Core Ops, SparseCore 0:
  22.6 52.4 all-gather.5
  77.2 51.2 all-gather.11
  130.6 89.4 all-gather.9
  221.7 31.2 all-gather.7
  254.5 32.0 all-gather.13
where the time goes:
time: 383 us; the launch traced here: 382 us
  waiting for transfers between devices  167 us (44%)
  matrix products  68.6 us (18%)
  local copies, waits for them, and re-layouts  48 us (13%)
  blocking collectives  42.2 us (11%)
  other arithmetic  27.9 us (7%)
  between operations  14.1 us (4%)
  starting transfers between devices  13.8 us (4%)
    all_to_all x1, waiting for transfers between devices, shards(): lax.all_to_all(bucket.reshape(owner_count, per_owner, kv_width), ('ctx',...  45.7 us
    all_gather x1, waiting for transfers between devices, shards(): lax.all_gather(value_cols, 'fsdp', axis=0, tiled=True)  41.8 us
    all_gather x1, waiting for transfers between devices, shards(): lax.all_gather(value_new, 'ctx', axis=0, tiled=True)  33.7 us
    dot_general x4, matrix products, attend_keys(): jnp.einsum('tkgs,skd->tkgd', weights.astype(jnp.bfloat16), heads_of_value...  30.7 us
    dot_general x4, matrix products, attend_keys(): jnp.einsum('tkgd,skd->tkgs', heads_of_query, heads_of_key, preferred_elem...  24.1 us
    all_gather x1, waiting for transfers between devices, shards(): lax.all_gather(key_cols, 'fsdp', axis=0, tiled=True)  23.9 us
    dot_general x2, local copies, waits for them, and re-layouts, project_rows(): jnp.dot(source, shard_rows, preferred_element_type=jnp.float32)  19 us
    reduce_sum x4, other arithmetic, attend_keys(): row_sum = row_sum * shrink + jnp.sum(weights, axis=-1)  17.9 us
  transfers between devices with their start and end apart: 7, of which 7 were waited for; matrix products, arithmetic and copies ran while one was open for 15% of the time, Pallas kernels for 0%

commit v1 on v0

--- a/solution.py
+++ b/solution.py
@@ -1,13 +1,25 @@
+import functools
 import math
 import jax
 import jax.numpy as jnp
 from jax import lax
 from jax.sharding import PartitionSpec as P
+from jax.lax import all_to_all, axis_size
 
 HEAD_WIDTH = 128
 EPSILON = 1e-06
 THETA = 1000000.0
 NEG_BIG = -1e30
+
+
+def order_pools_here(w_in, join_dim):
+    return jnp.concatenate(
+        all_to_all(jnp.stack(tuple((w_in for _ in range(axis_size("ctx"))))), "ctx", 0, 0),
+        axis=join_dim,
+    )
+
+
+render_loops = functools.partial(order_pools_here, join_dim=1)
 
 
 def norm_rope(projected, gain_vec, relative, head_size):
@@ -152,7 +164,7 @@
         return (positions, segment, relative)
 
     query_cols, key_cols, value_cols = (
-        lax.all_gather(w_query, "ctx", axis=1, tiled=True),
+        render_loops(w_query),
         lax.all_gather(w_key, "ctx", axis=1, tiled=True),
         lax.all_gather(w_value, "ctx", axis=1, tiled=True),
     )

time: 383 us -> 387 us (1.010)
  waiting for transfers between devices: 167 us -> 184 us
  local copies, waits for them, and re-layouts: 48 us -> 36.4 us
    all_gather x1 -> x0, blocking collectives: 14.4 us -> none  [shards(): lax.all_gather(w_query, 'ctx', axis=1, tiled=True)]
    all_gather x1, waiting for transfers between devices: 12.2 us -> 26 us  [shards(): lax.all_gather(key_new, 'ctx', axis=0, tiled=True)]
    all_to_all x0 -> x1, blocking collectives: none -> 13.4 us  [order_pools_here(): all_to_all(jnp.stack(tuple((w_in for _ in range(axis_size('ctx'))))), 'ct...]
    dot_general x2 -> x1, local copies, waits for them, and re-layouts: 19 us -> 6.5 us  [project_rows(): jnp.dot(source, shard_rows, preferred_element_type=jnp.float32)]
    all_gather x1, waiting for transfers between devices: 5.47 us -> 15.7 us  [shards(): lax.all_gather(query_cols, 'fsdp', axis=0, tiled=True)]
    all_to_all x1, waiting for transfers between devices: 45.7 us -> 39.2 us  [shards(): lax.all_to_all(bucket.reshape(owner_count, per_owner, kv_width), ('ctx',...]
  transfers between devices with their start and end apart: 7 -> 7, of which waited for: 7 -> 7; matrix products, arithmetic and copies ran while one was open for 15% -> 11% of each run, Pallas kernels for 0% -> 0%
where the time goes in v1:
time: 387 us; the launch traced here: 386 us
  waiting for transfers between devices  184 us (48%)
  matrix products  68.5 us (18%)
  blocking collectives  41.1 us (11%)
  local copies, waits for them, and re-layouts  36.4 us (9%)
  other arithmetic  27.9 us (7%)
  between operations  14.1 us (4%)
  starting transfers between devices  13.9 us (4%)
    all_gather x1, waiting for transfers between devices, shards(): lax.all_gather(value_cols, 'fsdp', axis=0, tiled=True)  41.8 us
    all_to_all x1, waiting for transfers between devices, shards(): lax.all_to_all(bucket.reshape(owner_count, per_owner, kv_width), ('ctx',...  39.2 us
    all_gather x1, waiting for transfers between devices, shards(): lax.all_gather(value_new, 'ctx', axis=0, tiled=True)  33.7 us
    dot_general x4, matrix products, attend_keys(): jnp.einsum('tkgs,skd->tkgd', weights.astype(jnp.bfloat16), heads_of_value...  30.5 us
    all_gather x1, waiting for transfers between devices, shards(): lax.all_gather(key_new, 'ctx', axis=0, tiled=True)  26 us
    dot_general x4, matrix products, attend_keys(): jnp.einsum('tkgd,skd->tkgs', heads_of_query, heads_of_key, preferred_elem...  24.1 us
    all_gather x1, waiting for transfers between devices, shards(): lax.all_gather(key_cols, 'fsdp', axis=0, tiled=True)  23.9 us
    reduce_sum x4, other arithmetic, attend_keys(): row_sum = row_sum * shrink + jnp.sum(weights, axis=-1)  17.9 us
  transfers between devices with their start and end apart: 7, of which 7 were waited for; matrix products, arithmetic and copies ran while one was open for 11% of the time, Pallas kernels for 0%

profile of v1, /device:TPU:1, one launch (start us, length us, event | category | flops | bytes accessed | tf_op | source)
XLA Modules:
  0.0 386.4 jit_solution(12697123467241126561)
XLA Ops:
  7.2 15.2 %all_gather.21 = bf16[128,1024]{1,0:T(8,128)(2,1)} all-gather(bf16[128,128]{1,0:T(8,128)(2,1)} %param.16), channel_id=1, replica_groups=mesh['ctx'=8,'fsdp'=16] {'ctx'}, dimensions={1}, use_global_device_ids=true | all-gather | bytes 294912 | tf_op jit(solution)/shard_map/all_gather | solution.py:168
  22.5 12.6 %all_gather.25 = bf16[128,1024]{1,0:T(8,128)(2,1)} all-gather(bf16[128,128]{1,0:T(8,128)(2,1)} %param.17), channel_id=1, replica_groups=mesh['ctx'=8,'fsdp'=16] {'ctx'}, dimensions={1}, use_global_device_ids=true | all-gather | bytes 294912 | tf_op jit(solution)/shard_map/all_gather | solution.py:169
  36.2 13.4 %all_to_all.19 = bf16[8,128,256]{1,2,0:T(8,128)(2,1)} all-to-all(bf16[8,128,256]{1,2,0:T(8,128)(2,1)S(1)} %stack.2), channel_id=1, replica_groups=mesh['ctx'=8,'fsdp'=16] {'ctx'}, dimensions={0} | all-to-all | bytes 1048576 | tf_op jit(solution)/shard_map/all_to_all | solution.py:17
  51.1 23.9 %all-gather.6.cloned.1.call-done = bf16[2048,1024]{1,0:T(8,128)(2,1)} async-done(((bf16[128,1024]{1,0:T(8,128)(2,1)}), bf16[2048,1024]{1,0:T(8,128)(2,1)}) %all-gather.6.cloned.1.call-update) | async-done | bytes 4194320 | tf_op jit(solution)/shard_map/all_gather | solution.py:175
  75.0 6.5 %copy.64 = bf16[1024,2048]{1,0:T(8,128)(2,1)} copy(bf16[1024,2048]{0,1:T(8,128)(2,1)} %bitcast.123) | data formatting | bytes 8388608 | tf_op jit(solution)/shard_map/dot_general | solution.py:118
  81.5 3.6 multiply_reduce_fusion.1
  86.7 41.8 %all-gather.12.cloned.1.call-done = bf16[2048,1024]{1,0:T(8,128)(2,1)} async-done(((bf16[128,1024]{1,0:T(8,128)(2,1)}), bf16[2048,1024]{1,0:T(8,128)(2,1)}) %all-gather.12.cloned.1.call-update) | async-done | bytes 4194320 | tf_op jit(solution)/shard_map/all_gather | solution.py:176
  128.4 4.3 %convolution_convert_fusion = bf16[256,1024]{1,0:T(8,128)(2,1)} fusion(bf16[2048,1024]{1,0:T(8,128)(2,1)} %all-gather.12.cloned.1.call-done, bf16[1,1,256,2048]{3,2,1,0:T(8,128)(2,1)S(1)} %copy-done.3, f32[2048]{0:T(1024)S(1)} %copy-done.9, f32[256]{0:T(256)S(1)} %add_rsqrt_fusion.2), kind=kOutput, calls=%fused_computation.37 | convolution fusion | flops 1076101120 | bytes 5776384 | tf_op jit(solution)/shard_map/dot_general | solution.py:118
  135.7 7.9 %all-to-all-start.1 = ((s32[128,1,4]{2,1,0:T(1,128)}), s32[128,1,4]{2,1,0:T(1,128)S(1)}, u32[]{:S(2)}, u32[]{:S(2)}) async-start(s32[128,1,4]{2,1,0:T(1,128)} %bitcast.28), calls=%async_computation.1 | async-start | bytes 131072 | tf_op jit(solution)/shard_map/all_to_all | solution.py:227
  143.6 3.3 scatter_custom_fusion.1
  146.9 2.2 reshape.395
  149.2 3.9 %all-to-all-done.1 = s32[128,1,4]{2,1,0:T(1,128)S(1)} async-done(((s32[128,1,4]{2,1,0:T(1,128)}), s32[128,1,4]{2,1,0:T(1,128)S(1)}, u32[]{:S(2)}, u32[]{:S(2)}) %all-to-all-start.1) | async-done | bytes 2080 | tf_op jit(solution)/shard_map/all_to_all | solution.py:227
  153.1 5.9 %all-to-all-start.2 = ((bf16[128,4,2048]{2,1,0:T(4,128)(2,1)}), bf16[128,4,2048]{2,1,0:T(4,128)(2,1)S(1)}, u32[]{:S(2)}, u32[]{:S(2)}) async-start(bf16[128,4,2048]{2,1,0:T(4,128)(2,1)} %reshape.395), calls=%async_computation.2 | async-start | bytes 4194304 | tf_op jit(solution)/shard_map/all_to_all | solution.py:220
  160.7 39.2 %all-to-all-done.2 = bf16[128,4,2048]{2,1,0:T(4,128)(2,1)S(1)} async-done(((bf16[128,4,2048]{2,1,0:T(4,128)(2,1)}), bf16[128,4,2048]{2,1,0:T(4,128)(2,1)S(1)}, u32[]{:S(2)}, u32[]{:S(2)}) %all-to-all-start.2) | async-done | bytes 2097184 | tf_op jit(solution)/shard_map/all_to_all | solution.py:220
  201.9 6.2 %scatter_custom_fusion.2 = bf16[512,2048]{1,0:T(8,128)(2,1)} fusion(s32[512]{0:T(512)S(1)} %bitcast.135, bf16[512,2048]{1,0:T(8,128)(2,1)} %reshape.418, bf16[]{:T(256)} %constant.129.clone.1), kind=kCustom, calls=%fused_computation.44 | custom fusion | bytes 2097664 | tf_op jit(solution)/shard_map/scatter | solution.py:238
  208.1 15.7 %all-gather.10.cloned.1.call-done = bf16[2048,2048]{0,1:T(8,128)(2,1)} async-done(((bf16[128,2048]{0,1:T(8,128)(2,1)}), bf16[2048,2048]{0,1:T(8,128)(2,1)}) %all-gather.10.cloned.1.call-update) | async-done | bytes 8388624 | tf_op jit(solution)/shard_map/all_gather | solution.py:174
  223.8 6.0 %multiply_reduce_fusion = (f32[256,16]{0,1:T(8,128)S(1)}, f32[256,16,128]{0,2,1:T(8,128)S(1)}) fusion(bf16[16,128,2048]{2,1,0:T(8,128)(2,1)} %bitcast.139, bf16[1,1,256,2048]{3,2,1,0:T(8,128)(2,1)S(1)} %copy-done.4, f32[2048]{0:T(1024)S(1)} %copy-done.9, f32[256]{0:T(256)S(1)} %add_rsqrt_fusion.2), kind=kOutput, calls=%fused_computation.36 | convolution fusion | flops 2150625280 | bytes 11559936 | tf_op jit(solution)/shard_map/dot_general | solution.py:118
  231.9 26.0 %all-gather.8.cloned.1.call-done = bf16[2048,1024]{1,0:T(8,128)(2,1)} async-done(((bf16[256,1024]{1,0:T(8,128)(2,1)}), bf16[2048,1024]{1,0:T(8,128)(2,1)}) %all-gather.8.cloned.1.call-update) | async-done | bytes 4194320 | tf_op jit(solution)/shard_map/all_gather | solution.py:188
  257.9 33.7 %all-gather.14.cloned.1.call-done = bf16[2048,1024]{1,0:T(8,128)(2,1)} async-done(((bf16[256,1024]{1,0:T(8,128)(2,1)}), bf16[2048,1024]{1,0:T(8,128)(2,1)}) %all-gather.14.cloned.1.call-update) | async-done | bytes 4194320 | tf_op jit(solution)/shard_map/all_gather | solution.py:189
  291.6 85.0 %while.15 = (s32[]{:T(128)}, f32[256,8,2]{0,2,1:T(2,128)S(1)}, f32[256,8,2]{0,2,1:T(2,128)S(1)}, f32[256,8,2,128]{0,3,2,1:T(8,128)}, s32[256]{0:T(256)S(1)}, /*i...) while((s32[]{:T(128)}, f32[256,8,2]{0,2,1:T(2,128)S(1)}, ...), condition=%wide.region_12.13_spmd.clone, body=%wide.region_9.12_spmd.clone.sunk | while | flops 1102991360 | bytes 41695372 | solution.py:95
  294.1 6.0 %fusion.72 = (f32[256,8,2]{0,2,1:T(2,128)S(1)}, f32[8,512,256,2]{2,1,3,0:T(8,128)}) fusion(pred[256,512]{0,1:T(8,128)(4,1)S(1)} %compare_and_fusion.2, bf16[512,8,128,1]{0,2,3,1:T(8,128)(2,1)S(1)} %bitcast.118, bf16[256,8,2,128]{3,0,2,1:T(8,128)(2,1)} %get-tuple-element.313), kind=kOutput, calls=%fused_computation.5.clone.1 | convolution fusion | flops 543158272 | bytes 10633216 | tf_op jit(solution)/shard_map/while/body/eval_jaxpr/tkgd,skd->tkgs/dot_general | solution.py:53
  300.1 4.5 %fusion.74 = f32[256,8,2]{0,2,1:T(2,128)S(1)} fusion(f32[8,512,256,2]{2,1,3,0:T(8,128)} %get-tuple-element.274, f32[256,8,2]{0,2,1:T(2,128)S(1)} %fusion.73, pred[256,512]{0,1:T(8,128)(4,1)S(1)} %compare_and_fusion.2), kind=kLoop, calls=%fused_computation.7.clone.1 | loop fusion | flops 10481664 | bytes 8552448 | tf_op jit(solution)/shard_map/while/body/eval_jaxpr/reduce_sum | solution.py:63
  305.2 7.2 %bitcast_add_fusion.3 = f32[256,8,2,128]{0,3,2,1:T(8,128)} fusion(f32[256,8,2,128]{0,3,2,1:T(8,128)} %get-tuple-element.294, bf16[512,8,128,1]{0,2,3,1:T(8,128)(2,1)S(1)} %bitcast.119, f32[8,512,256,2]{2,1,3,0:T(8,128)} %get-tuple-element.274, f32[256,8,2]{0,2,1:T(2,128)S(1)} %fusion.73, pred[256,512]{0,1:T(8,128)(4,1)S(1)} %compare_and_fusion.2, ...), kind=kOutput, calls=%fused_computation.10.clone.1 | convolution fusion | flops 548929536 | bytes 13795329 | tf_op jit(solution)/shard_map/while/body/eval_jaxpr/tkgs,skd->tkgd/dot_general | solution.py:64
  314.9 6.0 %fusion.72 = (f32[256,8,2]{0,2,1:T(2,128)S(1)}, f32[8,512,256,2]{2,1,3,0:T(8,128)}) fusion(pred[256,512]{0,1:T(8,128)(4,1)S(1)} %compare_and_fusion.2, bf16[512,8,128,1]{0,2,3,1:T(8,128)(2,1)S(1)} %bitcast.118, bf16[256,8,2,128]{3,0,2,1:T(8,128)(2,1)} %get-tuple-element.313), kind=kOutput, calls=%fused_computation.5.clone.1 | convolution fusion | flops 543158272 | bytes 10633216 | tf_op jit(solution)/shard_map/while/body/eval_jaxpr/tkgd,skd->tkgs/dot_general | solution.py:53
  320.9 4.5 %fusion.74 = f32[256,8,2]{0,2,1:T(2,128)S(1)} fusion(f32[8,512,256,2]{2,1,3,0:T(8,128)} %get-tuple-element.274, f32[256,8,2]{0,2,1:T(2,128)S(1)} %fusion.73, pred[256,512]{0,1:T(8,128)(4,1)S(1)} %compare_and_fusion.2), kind=kLoop, calls=%fused_computation.7.clone.1 | loop fusion | flops 10481664 | bytes 8552448 | tf_op jit(solution)/shard_map/while/body/eval_jaxpr/reduce_sum | solution.py:63
  326.0 7.8 %bitcast_add_fusion.3 = f32[256,8,2,128]{0,3,2,1:T(8,128)} fusion(f32[256,8,2,128]{0,3,2,1:T(8,128)} %get-tuple-element.294, bf16[512,8,128,1]{0,2,3,1:T(8,128)(2,1)S(1)} %bitcast.119, f32[8,512,256,2]{2,1,3,0:T(8,128)} %get-tuple-element.274, f32[256,8,2]{0,2,1:T(2,128)S(1)} %fusion.73, pred[256,512]{0,1:T(8,128)(4,1)S(1)} %compare_and_fusion.2, ...), kind=kOutput, calls=%fused_computation.10.clone.1 | convolution fusion | flops 548929536 | bytes 13795329 | tf_op jit(solution)/shard_map/while/body/eval_jaxpr/tkgs,skd->tkgd/dot_general | solution.py:64
  336.3 6.0 %fusion.72 = (f32[256,8,2]{0,2,1:T(2,128)S(1)}, f32[8,512,256,2]{2,1,3,0:T(8,128)}) fusion(pred[256,512]{0,1:T(8,128)(4,1)S(1)} %compare_and_fusion.2, bf16[512,8,128,1]{0,2,3,1:T(8,128)(2,1)S(1)} %bitcast.118, bf16[256,8,2,128]{3,0,2,1:T(8,128)(2,1)} %get-tuple-element.313), kind=kOutput, calls=%fused_computation.5.clone.1 | convolution fusion | flops 543158272 | bytes 10633216 | tf_op jit(solution)/shard_map/while/body/eval_jaxpr/tkgd,skd->tkgs/dot_general | solution.py:53
  342.3 4.5 %fusion.74 = f32[256,8,2]{0,2,1:T(2,128)S(1)} fusion(f32[8,512,256,2]{2,1,3,0:T(8,128)} %get-tuple-element.274, f32[256,8,2]{0,2,1:T(2,128)S(1)} %fusion.73, pred[256,512]{0,1:T(8,128)(4,1)S(1)} %compare_and_fusion.2), kind=kLoop, calls=%fused_computation.7.clone.1 | loop fusion | flops 10481664 | bytes 8552448 | tf_op jit(solution)/shard_map/while/body/eval_jaxpr/reduce_sum | solution.py:63
  347.4 7.8 %bitcast_add_fusion.3 = f32[256,8,2,128]{0,3,2,1:T(8,128)} fusion(f32[256,8,2,128]{0,3,2,1:T(8,128)} %get-tuple-element.294, bf16[512,8,128,1]{0,2,3,1:T(8,128)(2,1)S(1)} %bitcast.119, f32[8,512,256,2]{2,1,3,0:T(8,128)} %get-tuple-element.274, f32[256,8,2]{0,2,1:T(2,128)S(1)} %fusion.73, pred[256,512]{0,1:T(8,128)(4,1)S(1)} %compare_and_fusion.2, ...), kind=kOutput, calls=%fused_computation.10.clone.1 | convolution fusion | flops 548929536 | bytes 13795329 | tf_op jit(solution)/shard_map/while/body/eval_jaxpr/tkgs,skd->tkgd/dot_general | solution.py:64
  357.7 6.0 %fusion.72 = (f32[256,8,2]{0,2,1:T(2,128)S(1)}, f32[8,512,256,2]{2,1,3,0:T(8,128)}) fusion(pred[256,512]{0,1:T(8,128)(4,1)S(1)} %compare_and_fusion.2, bf16[512,8,128,1]{0,2,3,1:T(8,128)(2,1)S(1)} %bitcast.118, bf16[256,8,2,128]{3,0,2,1:T(8,128)(2,1)} %get-tuple-element.313), kind=kOutput, calls=%fused_computation.5.clone.1 | convolution fusion | flops 543158272 | bytes 10633216 | tf_op jit(solution)/shard_map/while/body/eval_jaxpr/tkgd,skd->tkgs/dot_general | solution.py:53
  363.7 4.5 %fusion.74 = f32[256,8,2]{0,2,1:T(2,128)S(1)} fusion(f32[8,512,256,2]{2,1,3,0:T(8,128)} %get-tuple-element.274, f32[256,8,2]{0,2,1:T(2,128)S(1)} %fusion.73, pred[256,512]{0,1:T(8,128)(4,1)S(1)} %compare_and_fusion.2), kind=kLoop, calls=%fused_computation.7.clone.1 | loop fusion | flops 10481664 | bytes 8552448 | tf_op jit(solution)/shard_map/while/body/eval_jaxpr/reduce_sum | solution.py:63
  368.8 7.8 %bitcast_add_fusion.3 = f32[256,8,2,128]{0,3,2,1:T(8,128)} fusion(f32[256,8,2,128]{0,3,2,1:T(8,128)} %get-tuple-element.294, bf16[512,8,128,1]{0,2,3,1:T(8,128)(2,1)S(1)} %bitcast.119, f32[8,512,256,2]{2,1,3,0:T(8,128)} %get-tuple-element.274, f32[256,8,2]{0,2,1:T(2,128)S(1)} %fusion.73, pred[256,512]{0,1:T(8,128)(4,1)S(1)} %compare_and_fusion.2, ...), kind=kOutput, calls=%fused_computation.10.clone.1 | convolution fusion | flops 548929536 | bytes 13795329 | tf_op jit(solution)/shard_map/while/body/eval_jaxpr/tkgs,skd->tkgd/dot_general | solution.py:64
  (117 shorter events, 28.5 us)
Async XLA Ops:
  7.2 42.5 %copy-start = (s32[16,8]{0,1:T(8,128)S(1)}, s32[16,8]{0,1:T(8,128)}, u32[]{:S(2)}) copy-start(s32[16,8]{0,1:T(8,128)} %param.21) | copy-start | bytes 1540
  7.2 42.7 %copy-start.6 = (s32[16,4]{0,1:T(4,128)S(1)}, s32[16,4]{0,1:T(4,128)}, u32[]{:S(2)}) copy-start(s32[16,4]{0,1:T(4,128)} %param.20) | copy-start | bytes 772
  7.2 43.3 %copy-start.3 = (bf16[1,1,256,2048]{3,2,1,0:T(8,128)(2,1)S(1)}, bf16[1,1,256,2048]{3,2,1,0:T(8,128)(2,1)}, u32[]{:S(2)}) copy-start(bf16[1,1,256,2048]{3,2,1,0:T(8,128)(2,1)} %param.13) | copy-start | bytes 3145732
  7.2 67.8 %all-gather.6.cloned.1.call-start = ((), (), s32[]{:S(2)}) async-start(), calls=%async_computation.3 | async-start | bytes 4456448 | tf_op jit(solution)/shard_map/all_gather | solution.py:175
  22.5 106.0 %all-gather.12.cloned.1.call-start = ((), (), s32[]{:S(2)}) async-start(), calls=%async_computation.6 | async-start | bytes 4456448 | tf_op jit(solution)/shard_map/all_gather | solution.py:176
  35.1 188.7 %all-gather.10.cloned.1.call-start = ((), (), s32[]{:S(2)}) async-start(), calls=%async_computation.5 | async-start | bytes 8912896 | tf_op jit(solution)/shard_map/all_gather | solution.py:174
  49.6 208.3 %all-gather.8.cloned.1.call-start = ((), (), s32[]{:S(2)}) async-start(), calls=%async_computation.4 | async-start | bytes 4718592 | tf_op jit(solution)/shard_map/all_gather | solution.py:188
  75.0 6.5 %copy-start.9 = (f32[2048]{0:T(1024)S(1)}, f32[2048]{0:T(1024)}, u32[]{:S(2)}) copy-start(f32[2048]{0:T(1024)} %param.14) | copy-start | bytes 24580
  81.5 3.6 copy-start.7
  86.6 46.2 %copy-start.5 = (s32[1,1,256]{2,1,0:T(1,128)S(1)}, s32[1,1,256]{2,1,0:T(1,128)}, u32[]{:S(2)}) copy-start(s32[1,1,256]{2,1,0:T(1,128)} %param.22) | copy-start | bytes 3076
  86.6 57.0 %copy-start.2 = (bf16[256,1024]{1,0:T(8,128)(2,1)S(1)}, bf16[256,1024]{1,0:T(8,128)(2,1)}, u32[]{:S(2)}) copy-start(bf16[256,1024]{1,0:T(8,128)(2,1)} %copy.65) | copy-start | bytes 1572868
  86.6 204.9 %all-gather.14.cloned.1.call-start = ((), (), s32[]{:S(2)}) async-start(), calls=%async_computation.7 | async-start | bytes 4718592 | tf_op jit(solution)/shard_map/all_gather | solution.py:189
  135.7 17.3 %all-to-all-start.1 = ((s32[128,1,4]{2,1,0:T(1,128)}), s32[128,1,4]{2,1,0:T(1,128)S(1)}, u32[]{:S(2)}, u32[]{:S(2)}) async-start(s32[128,1,4]{2,1,0:T(1,128)} %bitcast.28), calls=%async_computation.1 | async-start | bytes 131072 | tf_op jit(solution)/shard_map/all_to_all | solution.py:227
  153.1 46.8 %all-to-all-start.2 = ((bf16[128,4,2048]{2,1,0:T(4,128)(2,1)}), bf16[128,4,2048]{2,1,0:T(4,128)(2,1)S(1)}, u32[]{:S(2)}, u32[]{:S(2)}) async-start(bf16[128,4,2048]{2,1,0:T(4,128)(2,1)} %reshape.395), calls=%async_computation.2 | async-start | bytes 4194304 | tf_op jit(solution)/shard_map/all_to_all | solution.py:220
  201.9 21.9 %copy-start.4 = (bf16[1,1,256,2048]{3,2,1,0:T(8,128)(2,1)S(1)}, bf16[1,1,256,2048]{3,2,1,0:T(8,128)(2,1)}, u32[]{:S(2)}) copy-start(bf16[1,1,256,2048]{3,2,1,0:T(8,128)(2,1)} %param.13) | copy-start | bytes 3145732
  223.8 6.0 %copy-start.8 = (f32[128]{0:T(128)S(1)}, f32[128]{0:T(128)}, u32[]{:S(2)}) copy-start(f32[128]{0:T(128)} %param.18) | copy-start | bytes 1540
  376.6 3.2 copy-start.1
Sparse Core Ops, SparseCore 0:
  22.6 52.4 all-gather.5
  77.2 51.2 all-gather.11
  130.6 93.1 all-gather.9
  225.3 32.5 all-gather.7
  259.5 32.0 all-gather.13
